TPU v7x, 256 devices: a whole 4x4x8 slice. The times are simulated.
256 devices in a mesh: depth: 32 (over z, x_hi, core), shot: 8 (over y, x_lo).
Axes of the slice: x: 4 (x_hi: 2, x_lo: 2; x = x_hi * 2 + x_lo), y: 4, z: 8, core: 2. Of those that a mesh axis runs over, the one named last changes fastest.
Arguments:
- courant: float32 [512, 64, 128], P('depth'), may hold values from 0.04 to 0.2
- wave_before: float32 [8, 512, 64, 128], P('shot', 'depth'), may hold values from -10 to 10
- wave_current: float32 [8, 512, 64, 128], P('shot', 'depth'), may hold values from -10 to 10
- adjoint_after: float32 [8, 512, 64, 128], P('shot', 'depth'), may hold values from -10 to 10
- adjoint_current: float32 [8, 512, 64, 128], P('shot', 'depth'), may hold values from -10 to 10
- source_cell: int32 [8], P('shot'), may hold values from 0 to 4194303
- wavelet: float32 [8, 4], P('shot'), may hold values from -15 to 15
- receiver_cell: int32 [8, 256], P('shot'), may hold values from 0 to 4194303
- residual: float32 [8, 4, 256], P('shot'), may hold values from -12 to 12
- history: float32 [2, 5, 512, 64, 128], P(None, None, 'depth', 'shot'), may hold values from -23 to 23, as said below
Outputs:
- gradient: float32 [512, 64, 128], P('depth', 'shot')
- direction: float32 [512, 64, 128], P('depth', 'shot')
- courant_next: float32 [512, 64, 128], P('depth')
Inputs may be any that keep to these rules, and one draw needn't show every extreme that they name: In every pair the sum over all cells of history[0] times history[1] is positive.
All inputs are finite; a program needn't handle non-finite values.
Results may differ from a plain program's by a relative error of at most 0.00026.
Values sent between devices are 32-bit elements; how exact they have to be, the bound alone decides.
A program may use at most 128 MiB of HBM per device.

v0:
```python
import jax
import jax.numpy as jnp
from jax import lax
from jax.sharding import PartitionSpec as P

STEPS = 4
PAIRS = 5
coefficients = (-205.0 / 72.0, 8.0 / 5.0, -1.0 / 5.0, 8.0 / 315.0, -1.0 / 560.0)


def with_halo(cells, sides, width):
    for axis, dim in sides:
        count = lax.axis_size(axis)
        ends = count - 1
        head = lax.slice_in_dim(cells, 0, width, axis=dim)
        tail = lax.slice_in_dim(cells, cells.shape[dim] - width, cells.shape[dim], axis=dim)
        cells = jnp.concatenate(
            [
                lax.ppermute(tail, axis, [(i, (i + 1) % count) for i in range(ends)]),
                cells,
                lax.ppermute(head, axis, [((i + 1) % count, i) for i in range(ends)]),
            ],
            axis=dim,
        )
    return cells


def laplace_core(extended):
    interior = extended[4:-4]
    count_rows = interior.shape[0]
    width_x = interior.shape[1]
    width_y = interior.shape[2]
    padded = jnp.pad(interior, ((0, 0), (4, 4), (4, 4)))
    summed = 3.0 * coefficients[0] * interior
    for reach in range(1, 5):
        weight = coefficients[reach]
        summed = summed + weight * (
            extended[4 + reach : 4 + reach + count_rows]
            + extended[4 - reach : 4 - reach + count_rows]
        )
        summed = summed + weight * (
            padded[:, 4 + reach : 4 + reach + width_x, 4 : 4 + width_y]
            + padded[:, 4 - reach : 4 - reach + width_x, 4 : 4 + width_y]
        )
        summed = summed + weight * (
            padded[:, 4 : 4 + width_x, 4 + reach : 4 + reach + width_y]
            + padded[:, 4 : 4 + width_x, 4 - reach : 4 - reach + width_y]
        )
    return summed


def inject(volume, cell_ids, values, offset):
    count_rows = volume.shape[0]
    plane_size = volume.shape[1] * volume.shape[2]
    depth_row = cell_ids // plane_size - offset
    remainder = cell_ids % plane_size
    inside = (depth_row >= 0) & (depth_row < count_rows)
    row_safe = jnp.clip(depth_row, 0, count_rows - 1)
    return volume.at[row_safe, remainder // volume.shape[2], remainder % volume.shape[2]].add(
        jnp.where(inside, values, jnp.zeros_like(values))
    )


def per_device(
    courant,
    wave_before,
    wave_current,
    adjoint_after,
    adjoint_current,
    source_cell,
    wavelet,
    receiver_cell,
    residual,
    history,
):
    slab_rows = courant.shape[0]
    first_row = lax.axis_index("depth") * slab_rows
    shot_count = lax.axis_size("shot")
    summed = jnp.zeros(courant.shape, jnp.float32)
    laplacians = []
    wave_old = wave_before[0]
    wave_now = wave_current[0]
    for moment in range(STEPS):
        extended = with_halo(wave_now, (("depth", 0),), 4)
        laplacian = laplace_core(extended)
        wave_new = 2.0 * wave_now - wave_old + courant * laplacian
        wave_new = inject(wave_new, source_cell, wavelet[0, moment : moment + 1], first_row)
        laplacians.append(laplacian)
        wave_old, wave_now = (wave_now, wave_new)
    adjoint_old = adjoint_after[0]
    adjoint_now = adjoint_current[0]
    for moment in reversed(range(STEPS)):
        extended = with_halo(courant * adjoint_now, (("depth", 0),), 4)
        adjoint_new = 2.0 * adjoint_now - adjoint_old + laplace_core(extended)
        adjoint_new = inject(adjoint_new, receiver_cell[0], residual[0, moment], first_row)
        summed = summed + adjoint_new * laplacians[moment]
        adjoint_old, adjoint_now = (adjoint_now, adjoint_new)
    grad_piece = lax.psum_scatter(summed, "shot", scatter_dimension=1, tiled=True) * (
        1.0 / (shot_count * STEPS)
    )
    displaced = history[0]
    changes = history[1]
    step_change = jnp.einsum("izxy,jzxy->ij", displaced, changes, precision=lax.Precision.HIGHEST)
    change_change = jnp.einsum("izxy,jzxy->ij", changes, changes, precision=lax.Precision.HIGHEST)
    step_grad = jnp.sum(displaced * grad_piece, axis=(1, 2, 3))
    change_grad = jnp.sum(changes * grad_piece, axis=(1, 2, 3))
    packed = jnp.concatenate(
        [step_change, change_change, step_grad[None], change_grad[None]], axis=0
    )
    packed = lax.psum(packed, ("depth", "shot"))
    step_change = packed[:PAIRS]
    change_change = packed[PAIRS : 2 * PAIRS]
    step_grad = packed[2 * PAIRS]
    change_grad = packed[2 * PAIRS + 1]
    inverse = [1.0 / step_change[i, i] for i in range(PAIRS)]
    alphas = [None] * PAIRS
    for i in reversed(range(PAIRS)):
        value = step_grad[i]
        for j in range(i + 1, PAIRS):
            value = value - alphas[j] * step_change[i, j]
        alphas[i] = inverse[i] * value
    gamma = step_change[PAIRS - 1, PAIRS - 1] / change_change[PAIRS - 1, PAIRS - 1]
    gains = []
    for i in range(PAIRS):
        value = change_grad[i]
        for j in range(PAIRS):
            value = value - alphas[j] * change_change[i, j]
        value = gamma * value
        for j in range(i):
            value = value + gains[j] * step_change[j, i]
        gains.append(alphas[i] - inverse[i] * value)
    scaled = grad_piece
    for i in range(PAIRS):
        scaled = scaled - alphas[i] * changes[i]
    scaled = gamma * scaled
    for i in range(PAIRS):
        scaled = scaled + gains[i] * displaced[i]
    direction = -scaled
    piece_width = grad_piece.shape[1]
    own_courant = lax.dynamic_slice_in_dim(
        courant, lax.axis_index("shot") * piece_width, piece_width, 1
    )
    next_piece = own_courant + 0.05 * direction
    courant_next = lax.all_gather(next_piece, "shot", axis=1, tiled=True)
    return (grad_piece, direction, courant_next)


def solution(mesh):
    return jax.shard_map(
        per_device,
        mesh=mesh,
        in_specs=(
            P("depth", None, None),
            P("shot", "depth", None, None),
            P("shot", "depth", None, None),
            P("shot", "depth", None, None),
            P("shot", "depth", None, None),
            P("shot"),
            P("shot", None),
            P("shot", None),
            P("shot", None, None),
            P(None, None, "depth", "shot", None),
        ),
        out_specs=(P("depth", "shot", None), P("depth", "shot", None), P("depth", None, None)),
        check_vma=False,
    )
```

profile of v0, /device:TPU:32, one launch (start us, length us, event | category | flops | bytes accessed | tf_op | source)
XLA Modules:
  0.0 397.9 jit_solution(11437620847095359479)
XLA Ops:
  7.2 1.3 bitcast_multiply_fusion
  8.6 4.0 %collective-permute-start = (f32[4,64,128]{2,1,0:T(8,128)S(1)}, f32[4,64,128]{2,1,0:T(8,128)S(1)}, u32[]{:S(2)}, u32[]{:S(2)}) collective-permute-start(f32[4,64,128]{2,1,0:T(8,128)S(1)} %get-tuple-element.70), channel_id=1, source_target_pairs={{8,0},{16,8},{24,16},{32,24},{40,32},{48,40},{56,48},{64,56},{72,6... | collective-permute-start | bytes 393224 | tf_op jit(solution)/shard_map/ppermute | solution.py:21
  12.7 1.9 collective-permute-start.1
  14.7 6.0 %collective-permute-start.2 = (f32[4,64,128]{2,1,0:T(8,128)S(1)}, f32[4,64,128]{2,1,0:T(8,128)S(1)}, u32[]{:S(2)}, u32[]{:S(2)}) collective-permute-start(f32[4,64,128]{2,1,0:T(8,128)S(1)} %get-tuple-element.68), channel_id=1, source_target_pairs={{8,0},{16,8},{24,16},{32,24},{40,32},{48,40},{56,48},{64,56},{72,6... | collective-permute-start | bytes 393224 | tf_op jit(solution)/shard_map/ppermute | solution.py:21
  20.7 1.9 collective-permute-start.3
  23.3 0.7 fusion.369
  26.7 0.7 and_reduce_fusion
  27.4 1.9 fusion.184
  29.4 23.9 %scatter_fusion = f32[16,64,128]{2,1,0:T(8,128)S(1)} fusion(f32[16,64,128]{2,1,0:T(8,128)S(1)} %fusion.184, s32[256]{0:T(256)S(1)} %bitcast.180, f32[256]{0:T(256)} %get-tuple-element.128), kind=kCustom, calls=%fused_computation | custom fusion | flops 256 | bytes 6144 | tf_op jit(solution)/shard_map/scatter-add | solution.py:59
  53.4 3.7 fusion.348
  57.0 0.7 dynamic-slice.24
  59.8 6.1 %collective-permute-start.10 = (f32[4,64,128]{2,1,0:T(8,128)S(1)}, f32[4,64,128]{2,1,0:T(8,128)S(1)}, u32[]{:S(2)}, u32[]{:S(2)}) collective-permute-start(f32[4,64,128]{2,1,0:T(8,128)S(1)} %get-tuple-element.59), channel_id=1, source_target_pairs={{8,0},{16,8},{24,16},{32,24},{40,32},{48,40},{56,48},{64,56},{72,6... | collective-permute-start | bytes 393224 | tf_op jit(solution)/shard_map/ppermute | solution.py:21
  65.9 1.9 collective-permute-start.11
  67.8 0.7 fusion.363
  68.5 6.0 %collective-permute-start.4 = (f32[4,64,128]{2,1,0:T(8,128)}, f32[4,64,128]{2,1,0:T(8,128)S(1)}, u32[]{:S(2)}, u32[]{:S(2)}) collective-permute-start(f32[4,64,128]{2,1,0:T(8,128)} %get-tuple-element.66), channel_id=1, source_target_pairs={{8,0},{16,8},{24,16},{32,24},{40,32},{48,40},{56,48},{64,56},{72,6... | collective-permute-start | bytes 393224 | tf_op jit(solution)/shard_map/ppermute | solution.py:21
  74.5 1.9 collective-permute-start.5
  76.5 9.1 %fusion.59 = f32[16,64,128]{2,1,0:T(8,128)S(1)} fusion(f32[16,64,128]{2,1,0:T(8,128)} %copy-done.6, f32[4,64,128]{2,1,0:T(8,128)S(1)} %collective-permute-done.11, f32[4,64,128]{2,1,0:T(8,128)S(1)} %collective-permute-done.10, f32[1,16,64,128]{3,2,1,0:T(8,128)S(1)} %copy-done.2, f32[16,64,128]{2,1,0:T(8,128)S(1)} %scatter_fusion), kind=kLoop, calls=%fused_computation.289 | loop fusion | flops 6291456 | bytes 2359296 | tf_op jit(solution)/shard_map/add | solution.py:94
  85.6 15.2 %scatter_fusion.1 = f32[16,64,128]{2,1,0:T(8,128)S(1)} fusion(f32[16,64,128]{2,1,0:T(8,128)S(1)} %fusion.59, s32[256]{0:T(256)S(1)} %bitcast.181, f32[256]{0:T(256)S(1)} %get-tuple-element.127), kind=kCustom, calls=%fused_computation.1 | custom fusion | flops 256 | bytes 6144 | tf_op jit(solution)/shard_map/scatter-add | solution.py:59
  100.9 2.7 multiply_add_fusion.1
  103.6 6.1 %collective-permute-start.12 = (f32[4,64,128]{2,1,0:T(8,128)S(1)}, f32[4,64,128]{2,1,0:T(8,128)S(1)}, u32[]{:S(2)}, u32[]{:S(2)}) collective-permute-start(f32[4,64,128]{2,1,0:T(8,128)S(1)} %get-tuple-element.56), channel_id=1, source_target_pairs={{8,0},{16,8},{24,16},{32,24},{40,32},{48,40},{56,48},{64,56},{72,6... | collective-permute-start | bytes 393224 | tf_op jit(solution)/shard_map/ppermute | solution.py:21
  109.7 1.9 collective-permute-start.13
  111.6 0.6 dynamic-slice.25
  114.3 0.7 fusion.362
  115.0 6.0 %collective-permute-start.6 = (f32[4,64,128]{2,1,0:T(8,128)}, f32[4,64,128]{2,1,0:T(8,128)S(1)}, u32[]{:S(2)}, u32[]{:S(2)}) collective-permute-start(f32[4,64,128]{2,1,0:T(8,128)} %get-tuple-element.64), channel_id=1, source_target_pairs={{8,0},{16,8},{24,16},{32,24},{40,32},{48,40},{56,48},{64,56},{72,6... | collective-permute-start | bytes 393224 | tf_op jit(solution)/shard_map/ppermute | solution.py:21
  121.1 1.9 collective-permute-start.7
  123.0 2.0 fusion.34
  125.0 15.2 %scatter_fusion.2 = f32[16,64,128]{2,1,0:T(8,128)S(1)} fusion(f32[16,64,128]{2,1,0:T(8,128)S(1)} %fusion.34, s32[256]{0:T(256)S(1)} %bitcast.182, f32[256]{0:T(256)S(1)} %get-tuple-element.126), kind=kCustom, calls=%fused_computation.2 | custom fusion | flops 256 | bytes 6144 | tf_op jit(solution)/shard_map/scatter-add | solution.py:59
  140.2 10.6 %multiply_add_fusion = (f32[16,64,128]{2,1,0:T(8,128)S(1)}, f32[16,64,128]{2,1,0:T(8,128)}, f32[16,64,128]{2,1,0:T(8,128)S(1)}) fusion(f32[16,64,128]{2,1,0:T(8,128)S(1)} %copy-done, f32[16,64,128]{2,1,0:T(8,128)S(1)} %scatter-add.44, f32[16,64,128]{2,1,0:T(8,128)} %copy-done.3, f32[4,64,128]{2,1,0:T(8,128)} %collective-permute-done.7, ...), kind=kLoop, calls=%fused_computation.602 | loop fusion | flops 6553600 | bytes 3932160 | tf_op jit(solution)/shard_map/add | solution.py:86
  150.9 6.1 %collective-permute-start.14 = (f32[4,64,128]{2,1,0:T(8,128)S(1)}, f32[4,64,128]{2,1,0:T(8,128)S(1)}, u32[]{:S(2)}, u32[]{:S(2)}) collective-permute-start(f32[4,64,128]{2,1,0:T(8,128)S(1)} %get-tuple-element.53), channel_id=1, source_target_pairs={{8,0},{16,8},{24,16},{32,24},{40,32},{48,40},{56,48},{64,56},{72,6... | collective-permute-start | bytes 393224 | tf_op jit(solution)/shard_map/ppermute | solution.py:21
  156.9 2.1 collective-permute-start.15
  161.7 0.7 fusion.361
  162.4 6.0 %collective-permute-start.8 = (f32[4,64,128]{2,1,0:T(8,128)}, f32[4,64,128]{2,1,0:T(8,128)S(1)}, u32[]{:S(2)}, u32[]{:S(2)}) collective-permute-start(f32[4,64,128]{2,1,0:T(8,128)} %get-tuple-element.62), channel_id=1, source_target_pairs={{8,0},{16,8},{24,16},{32,24},{40,32},{48,40},{56,48},{64,56},{72,6... | collective-permute-start | bytes 393224 | tf_op jit(solution)/shard_map/ppermute | solution.py:21
  168.5 1.9 collective-permute-start.9
  170.4 2.2 fusion.9
  172.7 15.2 %scatter_fusion.3 = f32[16,64,128]{2,1,0:T(8,128)S(1)} fusion(f32[16,64,128]{2,1,0:T(8,128)S(1)} %fusion.9, s32[256]{0:T(256)S(1)} %bitcast.183, f32[256]{0:T(256)S(1)} %get-tuple-element.43), kind=kCustom, calls=%fused_computation.3 | custom fusion | flops 256 | bytes 6144 | tf_op jit(solution)/shard_map/scatter-add | solution.py:59
  187.9 3.9 fusion.87
  191.9 1.1 fusion.357
  193.0 1.2 convolution_bitcast_fusion
  194.2 1.4 convolution_bitcast_fusion.1
  195.6 48.2 %reduce-scatter.2.cloned.1.call-done = f32[16,8,128]{2,1,0:T(8,128)} async-done(((f32[16,64,128]{2,1,0:T(8,128)}), f32[16,8,128]{2,1,0:T(8,128)}) %reduce-scatter.2.cloned.1.call-update) | async-done | bytes 65552 | tf_op jit(solution)/shard_map/reduce_scatter | solution.py:98
  243.7 0.8 broadcast_multiply_fusion
  245.4 73.3 %psum.7 = f32[12,5]{0,1:T(8,128)S(1)} all-reduce(f32[12,5]{0,1:T(8,128)S(1)} %pad_maximum_fusion.16), channel_id=1, replica_groups=mesh['depth'=32,'shot'=8] {'depth','shot'}, use_global_device_ids=true, to_apply=%region_8.9 | all-reduce | flops 60 | bytes 480 | tf_op jit(solution)/shard_map/psum | solution.py:110
  318.8 0.7 fusion.366
  319.5 0.7 fusion.367
  320.2 0.7 fusion.365
  359.7 0.7 multiply_add_fusion.2
  360.4 29.8 %all_gather.3 = f32[16,64,128]{2,1,0:T(8,128)S(1)} all-gather(f32[16,8,128]{2,1,0:T(8,128)S(1)} %get-tuple-element.41), channel_id=1, replica_groups=mesh['depth'=32,'shot'=8] {'shot'}, dimensions={1}, use_global_device_ids=true | all-gather | bytes 589824 | tf_op jit(solution)/shard_map/all_gather | solution.py:144
  390.3 0.8 copy.49
  (70 shorter events, 2.7 us)
Async XLA Ops:
  7.2 236.6 %reduce-scatter.2.cloned.1.call-start = ((), (), s32[]{:S(2)}) async-start(), calls=%async_computation.1 | async-start | bytes 589824 | tf_op jit(solution)/shard_map/reduce_scatter | solution.py:98
  7.2 20.2 %copy-start.10 = (f32[1,16,64,128]{3,2,1,0:T(8,128)S(1)}, f32[1,16,64,128]{3,2,1,0:T(8,128)}, u32[]{:S(2)}) copy-start(f32[1,16,64,128]{3,2,1,0:T(8,128)} %param.19) | copy-start | bytes 1572868
  8.5 6.1 %copy-start.1 = (f32[1,16,64,128]{3,2,1,0:T(8,128)S(1)}, f32[1,16,64,128]{3,2,1,0:T(8,128)}, u32[]{:S(2)}) copy-start(f32[1,16,64,128]{3,2,1,0:T(8,128)} %param.18) | copy-start | bytes 1572868
  8.6 14.1 %copy-start.14 = (f32[1,4,256]{2,1,0:T(4,128)S(1)}, f32[1,4,256]{2,1,0:T(4,128)}, u32[]{:S(2)}) copy-start(f32[1,4,256]{2,1,0:T(4,128)} %param.24) | copy-start | bytes 12292
  8.6 14.1 %copy-start.15 = (s32[1,256]{1,0:T(1,128)S(1)}, s32[1,256]{1,0:T(1,128)}, u32[]{:S(2)}) copy-start(s32[1,256]{1,0:T(1,128)} %param.23) | copy-start | bytes 3076
  8.6 14.7 %copy-start.13 = (f32[1,4]{1,0:T(1,128)S(1)}, f32[1,4]{1,0:T(1,128)}, u32[]{:S(2)}) copy-start(f32[1,4]{1,0:T(1,128)} %param.22) | copy-start | bytes 52
  8.6 18.1 %copy-start.16 = (s32[3]{0:T(128)S(1)}, s32[3]{0:T(128)}, u32[]{:S(2)}) copy-start(s32[3]{0:T(128)} %constant.255.clone.1) | copy-start | bytes 40
  8.6 18.8 %copy-start.2 = (f32[1,16,64,128]{3,2,1,0:T(8,128)S(1)}, f32[1,16,64,128]{3,2,1,0:T(8,128)}, u32[]{:S(2)}) copy-start(f32[1,16,64,128]{3,2,1,0:T(8,128)} %param.20) | copy-start | bytes 1572868
  8.6 18.8 %collective-permute-start = (f32[4,64,128]{2,1,0:T(8,128)S(1)}, f32[4,64,128]{2,1,0:T(8,128)S(1)}, u32[]{:S(2)}, u32[]{:S(2)}) collective-permute-start(f32[4,64,128]{2,1,0:T(8,128)S(1)} %get-tuple-element.70), channel_id=1, source_target_pairs={{8,0},{16,8},{24,16},{32,24},{40,32},{48,40},{56,48},{64,56},{72,6... | collective-permute-start | bytes 393224 | tf_op jit(solution)/shard_map/ppermute | solution.py:21
  12.7 14.7 %collective-permute-start.1 = (f32[4,64,128]{2,1,0:T(8,128)S(1)}, f32[4,64,128]{2,1,0:T(8,128)S(1)}, u32[]{:S(2)}, u32[]{:S(2)}) collective-permute-start(f32[4,64,128]{2,1,0:T(8,128)S(1)} %get-tuple-element.71), channel_id=1, source_target_pairs={{0,8},{8,16},{16,24},{24,32},{32,40},{40,48},{48,56},{56,64},{64,7... | collective-permute-start | bytes 393224 | tf_op jit(solution)/shard_map/ppermute | solution.py:19
  14.7 38.7 %collective-permute-start.2 = (f32[4,64,128]{2,1,0:T(8,128)S(1)}, f32[4,64,128]{2,1,0:T(8,128)S(1)}, u32[]{:S(2)}, u32[]{:S(2)}) collective-permute-start(f32[4,64,128]{2,1,0:T(8,128)S(1)} %get-tuple-element.68), channel_id=1, source_target_pairs={{8,0},{16,8},{24,16},{32,24},{40,32},{48,40},{56,48},{64,56},{72,6... | collective-permute-start | bytes 393224 | tf_op jit(solution)/shard_map/ppermute | solution.py:21
  20.7 32.6 %collective-permute-start.3 = (f32[4,64,128]{2,1,0:T(8,128)S(1)}, f32[4,64,128]{2,1,0:T(8,128)S(1)}, u32[]{:S(2)}, u32[]{:S(2)}) collective-permute-start(f32[4,64,128]{2,1,0:T(8,128)S(1)} %get-tuple-element.69), channel_id=1, source_target_pairs={{0,8},{8,16},{16,24},{24,32},{32,40},{40,48},{48,56},{56,64},{64,7... | collective-permute-start | bytes 393224 | tf_op jit(solution)/shard_map/ppermute | solution.py:19
  29.4 24.0 %copy-start = (f32[16,64,128]{2,1,0:T(8,128)S(1)}, f32[16,64,128]{2,1,0:T(8,128)}, u32[]{:S(2)}) copy-start(f32[16,64,128]{2,1,0:T(8,128)} %param.16) | copy-start | bytes 1572868
  57.0 19.4 %copy-start.6 = (f32[16,64,128]{2,1,0:T(8,128)}, f32[16,64,128]{2,1,0:T(8,128)S(1)}, u32[]{:S(2)}) copy-start(f32[16,64,128]{2,1,0:T(8,128)S(1)} %get-tuple-element.61) | copy-start | bytes 1572868
  59.8 16.6 %collective-permute-start.10 = (f32[4,64,128]{2,1,0:T(8,128)S(1)}, f32[4,64,128]{2,1,0:T(8,128)S(1)}, u32[]{:S(2)}, u32[]{:S(2)}) collective-permute-start(f32[4,64,128]{2,1,0:T(8,128)S(1)} %get-tuple-element.59), channel_id=1, source_target_pairs={{8,0},{16,8},{24,16},{32,24},{40,32},{48,40},{56,48},{64,56},{72,6... | collective-permute-start | bytes 393224 | tf_op jit(solution)/shard_map/ppermute | solution.py:21
  65.9 10.6 %collective-permute-start.11 = (f32[4,64,128]{2,1,0:T(8,128)S(1)}, f32[4,64,128]{2,1,0:T(8,128)S(1)}, u32[]{:S(2)}, u32[]{:S(2)}) collective-permute-start(f32[4,64,128]{2,1,0:T(8,128)S(1)} %get-tuple-element.60), channel_id=1, source_target_pairs={{0,8},{8,16},{16,24},{24,32},{32,40},{40,48},{48,56},{56,64},{64,7... | collective-permute-start | bytes 393224 | tf_op jit(solution)/shard_map/ppermute | solution.py:19
  68.5 32.4 %collective-permute-start.4 = (f32[4,64,128]{2,1,0:T(8,128)}, f32[4,64,128]{2,1,0:T(8,128)S(1)}, u32[]{:S(2)}, u32[]{:S(2)}) collective-permute-start(f32[4,64,128]{2,1,0:T(8,128)} %get-tuple-element.66), channel_id=1, source_target_pairs={{8,0},{16,8},{24,16},{32,24},{40,32},{48,40},{56,48},{64,56},{72,6... | collective-permute-start | bytes 393224 | tf_op jit(solution)/shard_map/ppermute | solution.py:21
  74.5 26.3 %collective-permute-start.5 = (f32[4,64,128]{2,1,0:T(8,128)S(1)}, f32[4,64,128]{2,1,0:T(8,128)S(1)}, u32[]{:S(2)}, u32[]{:S(2)}) collective-permute-start(f32[4,64,128]{2,1,0:T(8,128)S(1)} %get-tuple-element.67), channel_id=1, source_target_pairs={{0,8},{8,16},{16,24},{24,32},{32,40},{40,48},{48,56},{56,64},{64,7... | collective-permute-start | bytes 393224 | tf_op jit(solution)/shard_map/ppermute | solution.py:19
  103.6 9.3 %copy-start.7 = (f32[16,64,128]{2,1,0:T(8,128)}, f32[16,64,128]{2,1,0:T(8,128)S(1)}, u32[]{:S(2)}) copy-start(f32[16,64,128]{2,1,0:T(8,128)S(1)} %get-tuple-element.58) | copy-start | bytes 1572868
  103.6 19.4 %collective-permute-start.12 = (f32[4,64,128]{2,1,0:T(8,128)S(1)}, f32[4,64,128]{2,1,0:T(8,128)S(1)}, u32[]{:S(2)}, u32[]{:S(2)}) collective-permute-start(f32[4,64,128]{2,1,0:T(8,128)S(1)} %get-tuple-element.56), channel_id=1, source_target_pairs={{8,0},{16,8},{24,16},{32,24},{40,32},{48,40},{56,48},{64,56},{72,6... | collective-permute-start | bytes 393224 | tf_op jit(solution)/shard_map/ppermute | solution.py:21
  109.7 13.3 %collective-permute-start.13 = (f32[4,64,128]{2,1,0:T(8,128)S(1)}, f32[4,64,128]{2,1,0:T(8,128)S(1)}, u32[]{:S(2)}, u32[]{:S(2)}) collective-permute-start(f32[4,64,128]{2,1,0:T(8,128)S(1)} %get-tuple-element.57), channel_id=1, source_target_pairs={{0,8},{8,16},{16,24},{24,32},{32,40},{40,48},{48,56},{56,64},{64,7... | collective-permute-start | bytes 393224 | tf_op jit(solution)/shard_map/ppermute | solution.py:19
  114.3 10.7 %copy-start.3 = (f32[16,64,128]{2,1,0:T(8,128)}, f32[16,64,128]{2,1,0:T(8,128)S(1)}, u32[]{:S(2)}) copy-start(f32[16,64,128]{2,1,0:T(8,128)S(1)} %scatter-add.45) | copy-start | bytes 1572868
  114.3 8.7 %copy-start.8 = (f32[16,64,128]{2,1,0:T(8,128)S(1)}, f32[16,64,128]{2,1,0:T(8,128)}, u32[]{:S(2)}) copy-start(f32[16,64,128]{2,1,0:T(8,128)} %copy-done.7) | copy-start | bytes 1572868
  115.0 25.2 %collective-permute-start.6 = (f32[4,64,128]{2,1,0:T(8,128)}, f32[4,64,128]{2,1,0:T(8,128)S(1)}, u32[]{:S(2)}, u32[]{:S(2)}) collective-permute-start(f32[4,64,128]{2,1,0:T(8,128)} %get-tuple-element.64), channel_id=1, source_target_pairs={{8,0},{16,8},{24,16},{32,24},{40,32},{48,40},{56,48},{64,56},{72,6... | collective-permute-start | bytes 393224 | tf_op jit(solution)/shard_map/ppermute | solution.py:21
  121.1 19.2 %collective-permute-start.7 = (f32[4,64,128]{2,1,0:T(8,128)}, f32[4,64,128]{2,1,0:T(8,128)}, u32[]{:S(2)}, u32[]{:S(2)}) collective-permute-start(f32[4,64,128]{2,1,0:T(8,128)} %get-tuple-element.65), channel_id=1, source_target_pairs={{0,8},{8,16},{16,24},{24,32},{32,40},{40,48},{48,56},{56,64},{64,7... | collective-permute-start | bytes 393224 | tf_op jit(solution)/shard_map/ppermute | solution.py:19
  150.8 9.5 %copy-start.4 = (f32[16,64,128]{2,1,0:T(8,128)}, f32[16,64,128]{2,1,0:T(8,128)S(1)}, u32[]{:S(2)}) copy-start(f32[16,64,128]{2,1,0:T(8,128)S(1)} %get-tuple-element.55) | copy-start | bytes 1572868
  150.9 19.6 %collective-permute-start.14 = (f32[4,64,128]{2,1,0:T(8,128)S(1)}, f32[4,64,128]{2,1,0:T(8,128)S(1)}, u32[]{:S(2)}, u32[]{:S(2)}) collective-permute-start(f32[4,64,128]{2,1,0:T(8,128)S(1)} %get-tuple-element.53), channel_id=1, source_target_pairs={{8,0},{16,8},{24,16},{32,24},{40,32},{48,40},{56,48},{64,56},{72,6... | collective-permute-start | bytes 393224 | tf_op jit(solution)/shard_map/ppermute | solution.py:21
  156.9 13.5 %collective-permute-start.15 = (f32[4,64,128]{2,1,0:T(8,128)S(1)}, f32[4,64,128]{2,1,0:T(8,128)}, u32[]{:S(2)}, u32[]{:S(2)}) collective-permute-start(f32[4,64,128]{2,1,0:T(8,128)S(1)} %get-tuple-element.54), channel_id=1, source_target_pairs={{0,8},{8,16},{16,24},{24,32},{32,40},{40,48},{48,56},{56,64},{64,7... | collective-permute-start | bytes 393224 | tf_op jit(solution)/shard_map/ppermute | solution.py:19
  161.7 8.7 %copy-start.5 = (f32[16,64,128]{2,1,0:T(8,128)S(1)}, f32[16,64,128]{2,1,0:T(8,128)}, u32[]{:S(2)}) copy-start(f32[16,64,128]{2,1,0:T(8,128)} %copy-done.4) | copy-start | bytes 1572868
  162.4 25.5 %collective-permute-start.8 = (f32[4,64,128]{2,1,0:T(8,128)}, f32[4,64,128]{2,1,0:T(8,128)S(1)}, u32[]{:S(2)}, u32[]{:S(2)}) collective-permute-start(f32[4,64,128]{2,1,0:T(8,128)} %get-tuple-element.62), channel_id=1, source_target_pairs={{8,0},{16,8},{24,16},{32,24},{40,32},{48,40},{56,48},{64,56},{72,6... | collective-permute-start | bytes 393224 | tf_op jit(solution)/shard_map/ppermute | solution.py:21
  168.5 19.4 %collective-permute-start.9 = (f32[4,64,128]{2,1,0:T(8,128)}, f32[4,64,128]{2,1,0:T(8,128)S(1)}, u32[]{:S(2)}, u32[]{:S(2)}) collective-permute-start(f32[4,64,128]{2,1,0:T(8,128)} %get-tuple-element.63), channel_id=1, source_target_pairs={{0,8},{8,16},{16,24},{24,32},{32,40},{40,48},{48,56},{56,64},{64,7... | collective-permute-start | bytes 393224 | tf_op jit(solution)/shard_map/ppermute | solution.py:19
  244.6 111.4 %copy-start.12 = (f32[16,8,128]{2,1,0:T(8,128)}, f32[16,8,128]{2,1,0:T(8,128)S(1)}, u32[]{:S(2)}) copy-start(f32[16,8,128]{2,1,0:T(8,128)S(1)} %broadcast_multiply_fusion) | copy-start | bytes 196612
  244.6 115.1 %copy-start.9 = (f32[2,5,16,8,128]{4,3,2,1,0:T(8,128)S(1)}, f32[2,5,16,8,128]{4,3,2,1,0:T(8,128)}, u32[]{:S(2)}) copy-start(f32[2,5,16,8,128]{4,3,2,1,0:T(8,128)} %param.25) | copy-start | bytes 1966084
  244.6 115.1 %copy-start.11 = (f32[16,8,128]{2,1,0:T(8,128)S(1)}, f32[16,8,128]{2,1,0:T(8,128)}, u32[]{:S(2)}) copy-start(f32[16,8,128]{2,1,0:T(8,128)} %reduce-scatter.2.cloned.1.call-done) | copy-start | bytes 196612
Sparse Core Ops, SparseCore 0:
  192.0 51.6 reduce-scatter.1
where the time goes:
time: 400 us; the launch traced here: 398 us
  other arithmetic  111 us (28%)
  blocking collectives  103 us (26%)
  starting transfers between devices  61.9 us (15%)
  between operations  61.9 us (15%)
  waiting for transfers between devices  48.2 us (12%)
  local copies, waits for them, and re-layouts  9.48 us (2%)
    psum x1, blocking collectives, per_device(): packed = lax.psum(packed, ('depth', 'shot'))  73.3 us
    scatter-add x4, other arithmetic, inject(): volume.at[row_safe, remainder // volume.shape[2], remainder % volume.shap...  69.6 us
    reduce_scatter x1, waiting for transfers between devices, per_device(): lax.psum_scatter(summed, 'shot', scatter_dimension=1, tiled=True)  48.2 us
    ppermute x8, starting transfers between devices, with_halo(): lax.ppermute(head, axis, [((i + 1) % count, i) for i in range(ends)])  46.4 us
    all_gather x1, blocking collectives, per_device(): courant_next = lax.all_gather(next_piece, 'shot', axis=1, tiled=True)  29.8 us
    add x3, other arithmetic, per_device(): wave_new = 2.0 * wave_now - wave_old + courant * laplacian  17 us
    ppermute x8, starting transfers between devices, with_halo(): lax.ppermute(tail, axis, [(i, (i + 1) % count) for i in range(ends)])  15.5 us
    add x4, other arithmetic, per_device(): adjoint_new = 2.0 * adjoint_now - adjoint_old + laplace_core(extended)  15.3 us
  transfers between devices with their start and end apart: 17, of which 1 were waited for; matrix products, arithmetic and copies ran while one was open for 24% of the time, Pallas kernels for 0%

commit v1 on v0

--- a/solution.py
+++ b/solution.py
@@ -141,7 +141,9 @@
         courant, lax.axis_index("shot") * piece_width, piece_width, 1
     )
     next_piece = own_courant + 0.05 * direction
-    courant_next = lax.all_gather(next_piece, "shot", axis=1, tiled=True)
+    courant_next = jnp.concatenate(
+        lax.all_to_all(jnp.stack([next_piece] * lax.axis_size("shot")), "shot", 0, 0), axis=1
+    )
     return (grad_piece, direction, courant_next)
 
 

time: 400 us -> 384 us (0.960)
  blocking collectives: 103 us -> 87.1 us
    all_gather x1 -> x0, blocking collectives: 29.8 us -> none  [per_device(): courant_next = lax.all_gather(next_piece, 'shot', axis=1, tiled=True)]
    all_to_all x0 -> x1, blocking collectives: none -> 13.7 us  [per_device(): lax.all_to_all(jnp.stack([next_piece] * lax.axis_size('shot')), 'shot', 0...]
  transfers between devices with their start and end apart: 17 -> 17, of which waited for: 1 -> 1; matrix products, arithmetic and copies ran while one was open for 24% -> 25% of each run, Pallas kernels for 0% -> 0%
where the time goes in v1:
time: 384 us; the launch traced here: 382 us
  other arithmetic  111 us (29%)
  blocking collectives  87.1 us (23%)
  between operations  62 us (16%)
  starting transfers between devices  61.9 us (16%)
  waiting for transfers between devices  48.2 us (13%)
  local copies, waits for them, and re-layouts  9.57 us (2%)
    psum x1, blocking collectives, per_device(): packed = lax.psum(packed, ('depth', 'shot'))  73.3 us
    scatter-add x4, other arithmetic, inject(): volume.at[row_safe, remainder // volume.shape[2], remainder % volume.shap...  69.6 us
    reduce_scatter x1, waiting for transfers between devices, per_device(): lax.psum_scatter(summed, 'shot', scatter_dimension=1, tiled=True)  48.2 us
    ppermute x8, starting transfers between devices, with_halo(): lax.ppermute(head, axis, [((i + 1) % count, i) for i in range(ends)])  46.4 us
    add x3, other arithmetic, per_device(): wave_new = 2.0 * wave_now - wave_old + courant * laplacian  17 us
    ppermute x8, starting transfers between devices, with_halo(): lax.ppermute(tail, axis, [(i, (i + 1) % count) for i in range(ends)])  15.5 us
    add x4, other arithmetic, per_device(): adjoint_new = 2.0 * adjoint_now - adjoint_old + laplace_core(extended)  15.3 us
    all_to_all x1, blocking collectives, per_device(): lax.all_to_all(jnp.stack([next_piece] * lax.axis_size('shot')), 'shot', 0...  13.7 us
  transfers between devices with their start and end apart: 17, of which 1 were waited for; matrix products, arithmetic and copies ran while one was open for 25% of the time, Pallas kernels for 0%

profile of v1, /device:TPU:32, one launch (start us, length us, event | category | flops | bytes accessed | tf_op | source)
XLA Modules:
  0.0 381.9 jit_solution(1393123424275851371)
XLA Ops:
  7.2 1.3 bitcast_multiply_fusion
  8.6 4.0 %collective-permute-start = (f32[4,64,128]{2,1,0:T(8,128)S(1)}, f32[4,64,128]{2,1,0:T(8,128)S(1)}, u32[]{:S(2)}, u32[]{:S(2)}) collective-permute-start(f32[4,64,128]{2,1,0:T(8,128)S(1)} %get-tuple-element.70), channel_id=1, source_target_pairs={{8,0},{16,8},{24,16},{32,24},{40,32},{48,40},{56,48},{64,56},{72,6... | collective-permute-start | bytes 393224 | tf_op jit(solution)/shard_map/ppermute | solution.py:21
  12.7 1.9 collective-permute-start.1
  14.7 6.0 %collective-permute-start.2 = (f32[4,64,128]{2,1,0:T(8,128)S(1)}, f32[4,64,128]{2,1,0:T(8,128)S(1)}, u32[]{:S(2)}, u32[]{:S(2)}) collective-permute-start(f32[4,64,128]{2,1,0:T(8,128)S(1)} %get-tuple-element.68), channel_id=1, source_target_pairs={{8,0},{16,8},{24,16},{32,24},{40,32},{48,40},{56,48},{64,56},{72,6... | collective-permute-start | bytes 393224 | tf_op jit(solution)/shard_map/ppermute | solution.py:21
  20.7 1.9 collective-permute-start.3
  23.3 0.7 fusion.369
  26.7 0.7 and_reduce_fusion
  27.4 1.9 fusion.184
  29.4 23.9 %scatter_fusion = f32[16,64,128]{2,1,0:T(8,128)S(1)} fusion(f32[16,64,128]{2,1,0:T(8,128)S(1)} %fusion.184, s32[256]{0:T(256)S(1)} %bitcast.185, f32[256]{0:T(256)} %get-tuple-element.128), kind=kCustom, calls=%fused_computation | custom fusion | flops 256 | bytes 6144 | tf_op jit(solution)/shard_map/scatter-add | solution.py:59
  53.4 3.7 fusion.348
  57.0 0.7 dynamic-slice.24
  59.8 6.1 %collective-permute-start.10 = (f32[4,64,128]{2,1,0:T(8,128)S(1)}, f32[4,64,128]{2,1,0:T(8,128)S(1)}, u32[]{:S(2)}, u32[]{:S(2)}) collective-permute-start(f32[4,64,128]{2,1,0:T(8,128)S(1)} %get-tuple-element.59), channel_id=1, source_target_pairs={{8,0},{16,8},{24,16},{32,24},{40,32},{48,40},{56,48},{64,56},{72,6... | collective-permute-start | bytes 393224 | tf_op jit(solution)/shard_map/ppermute | solution.py:21
  65.9 1.9 collective-permute-start.11
  67.8 0.7 fusion.363
  68.5 6.0 %collective-permute-start.4 = (f32[4,64,128]{2,1,0:T(8,128)}, f32[4,64,128]{2,1,0:T(8,128)S(1)}, u32[]{:S(2)}, u32[]{:S(2)}) collective-permute-start(f32[4,64,128]{2,1,0:T(8,128)} %get-tuple-element.66), channel_id=1, source_target_pairs={{8,0},{16,8},{24,16},{32,24},{40,32},{48,40},{56,48},{64,56},{72,6... | collective-permute-start | bytes 393224 | tf_op jit(solution)/shard_map/ppermute | solution.py:21
  74.5 1.9 collective-permute-start.5
  76.5 9.1 %fusion.59 = f32[16,64,128]{2,1,0:T(8,128)S(1)} fusion(f32[16,64,128]{2,1,0:T(8,128)} %copy-done.6, f32[4,64,128]{2,1,0:T(8,128)S(1)} %collective-permute-done.11, f32[4,64,128]{2,1,0:T(8,128)S(1)} %collective-permute-done.10, f32[1,16,64,128]{3,2,1,0:T(8,128)S(1)} %copy-done.2, f32[16,64,128]{2,1,0:T(8,128)S(1)} %scatter_fusion), kind=kLoop, calls=%fused_computation.289 | loop fusion | flops 6291456 | bytes 2359296 | tf_op jit(solution)/shard_map/add | solution.py:94
  85.6 15.2 %scatter_fusion.1 = f32[16,64,128]{2,1,0:T(8,128)S(1)} fusion(f32[16,64,128]{2,1,0:T(8,128)S(1)} %fusion.59, s32[256]{0:T(256)S(1)} %bitcast.186, f32[256]{0:T(256)S(1)} %get-tuple-element.127), kind=kCustom, calls=%fused_computation.1 | custom fusion | flops 256 | bytes 6144 | tf_op jit(solution)/shard_map/scatter-add | solution.py:59
  100.9 2.7 multiply_add_fusion.1
  103.6 6.1 %collective-permute-start.12 = (f32[4,64,128]{2,1,0:T(8,128)S(1)}, f32[4,64,128]{2,1,0:T(8,128)S(1)}, u32[]{:S(2)}, u32[]{:S(2)}) collective-permute-start(f32[4,64,128]{2,1,0:T(8,128)S(1)} %get-tuple-element.56), channel_id=1, source_target_pairs={{8,0},{16,8},{24,16},{32,24},{40,32},{48,40},{56,48},{64,56},{72,6... | collective-permute-start | bytes 393224 | tf_op jit(solution)/shard_map/ppermute | solution.py:21
  109.7 1.9 collective-permute-start.13
  111.6 0.6 dynamic-slice.25
  114.3 0.7 fusion.362
  115.0 6.0 %collective-permute-start.6 = (f32[4,64,128]{2,1,0:T(8,128)}, f32[4,64,128]{2,1,0:T(8,128)S(1)}, u32[]{:S(2)}, u32[]{:S(2)}) collective-permute-start(f32[4,64,128]{2,1,0:T(8,128)} %get-tuple-element.64), channel_id=1, source_target_pairs={{8,0},{16,8},{24,16},{32,24},{40,32},{48,40},{56,48},{64,56},{72,6... | collective-permute-start | bytes 393224 | tf_op jit(solution)/shard_map/ppermute | solution.py:21
  121.1 1.9 collective-permute-start.7
  123.0 2.0 fusion.34
  125.0 15.2 %scatter_fusion.2 = f32[16,64,128]{2,1,0:T(8,128)S(1)} fusion(f32[16,64,128]{2,1,0:T(8,128)S(1)} %fusion.34, s32[256]{0:T(256)S(1)} %bitcast.187, f32[256]{0:T(256)S(1)} %get-tuple-element.126), kind=kCustom, calls=%fused_computation.2 | custom fusion | flops 256 | bytes 6144 | tf_op jit(solution)/shard_map/scatter-add | solution.py:59
  140.2 10.6 %multiply_add_fusion = (f32[16,64,128]{2,1,0:T(8,128)S(1)}, f32[16,64,128]{2,1,0:T(8,128)}, f32[16,64,128]{2,1,0:T(8,128)S(1)}) fusion(f32[16,64,128]{2,1,0:T(8,128)S(1)} %copy-done, f32[16,64,128]{2,1,0:T(8,128)S(1)} %scatter-add.44, f32[16,64,128]{2,1,0:T(8,128)} %copy-done.3, f32[4,64,128]{2,1,0:T(8,128)} %collective-permute-done.7, ...), kind=kLoop, calls=%fused_computation.603 | loop fusion | flops 6553600 | bytes 3932160 | tf_op jit(solution)/shard_map/add | solution.py:86
  150.9 6.1 %collective-permute-start.14 = (f32[4,64,128]{2,1,0:T(8,128)S(1)}, f32[4,64,128]{2,1,0:T(8,128)S(1)}, u32[]{:S(2)}, u32[]{:S(2)}) collective-permute-start(f32[4,64,128]{2,1,0:T(8,128)S(1)} %get-tuple-element.53), channel_id=1, source_target_pairs={{8,0},{16,8},{24,16},{32,24},{40,32},{48,40},{56,48},{64,56},{72,6... | collective-permute-start | bytes 393224 | tf_op jit(solution)/shard_map/ppermute | solution.py:21
  156.9 2.1 collective-permute-start.15
  161.7 0.7 fusion.361
  162.4 6.0 %collective-permute-start.8 = (f32[4,64,128]{2,1,0:T(8,128)}, f32[4,64,128]{2,1,0:T(8,128)S(1)}, u32[]{:S(2)}, u32[]{:S(2)}) collective-permute-start(f32[4,64,128]{2,1,0:T(8,128)} %get-tuple-element.62), channel_id=1, source_target_pairs={{8,0},{16,8},{24,16},{32,24},{40,32},{48,40},{56,48},{64,56},{72,6... | collective-permute-start | bytes 393224 | tf_op jit(solution)/shard_map/ppermute | solution.py:21
  168.5 1.9 collective-permute-start.9
  170.4 2.2 fusion.9
  172.7 15.2 %scatter_fusion.3 = f32[16,64,128]{2,1,0:T(8,128)S(1)} fusion(f32[16,64,128]{2,1,0:T(8,128)S(1)} %fusion.9, s32[256]{0:T(256)S(1)} %bitcast.188, f32[256]{0:T(256)S(1)} %get-tuple-element.43), kind=kCustom, calls=%fused_computation.3 | custom fusion | flops 256 | bytes 6144 | tf_op jit(solution)/shard_map/scatter-add | solution.py:59
  187.9 3.9 %fusion.87 = f32[16,64,128]{2,1,0:T(8,128)} fusion(f32[16,64,128]{2,1,0:T(8,128)S(1)} %scatter_fusion, f32[16,64,128]{2,1,0:T(8,128)S(1)} %scatter-add.46, f32[4,64,128]{2,1,0:T(8,128)S(1)} %collective-permute-done.9, f32[4,64,128]{2,1,0:T(8,128)S(1)} %collective-permute-done.8, f32[16,64,128]{2,1,0:T(8,128)S(1)} %scatter_fusion.3, ...), kind=kLoop, calls=%fused_computation.317 | loop fusion | flops 6815744 | bytes 4980736 | tf_op jit(solution)/shard_map/add | solution.py:96
  191.9 1.1 fusion.357
  193.0 1.2 convolution_bitcast_fusion
  194.2 1.4 convolution_bitcast_fusion.1
  195.6 48.2 %reduce-scatter.2.cloned.1.call-done = f32[16,8,128]{2,1,0:T(8,128)} async-done(((f32[16,64,128]{2,1,0:T(8,128)}), f32[16,8,128]{2,1,0:T(8,128)}) %reduce-scatter.2.cloned.1.call-update) | async-done | bytes 65552 | tf_op jit(solution)/shard_map/reduce_scatter | solution.py:98
  243.7 0.8 broadcast_multiply_fusion
  245.4 73.3 %psum.7 = f32[12,5]{0,1:T(8,128)S(1)} all-reduce(f32[12,5]{0,1:T(8,128)S(1)} %pad_maximum_fusion.16), channel_id=1, replica_groups=mesh['depth'=32,'shot'=8] {'depth','shot'}, use_global_device_ids=true, to_apply=%region_8.9 | all-reduce | flops 60 | bytes 480 | tf_op jit(solution)/shard_map/psum | solution.py:110
  318.8 0.7 fusion.366
  319.5 0.7 fusion.367
  320.2 0.7 fusion.365
  359.7 0.7 multiply_add_fusion.2
  360.5 13.7 %all_to_all.5 = f32[8,16,8,128]{3,2,1,0:T(8,128)S(1)} all-to-all(f32[8,16,8,128]{3,2,1,0:T(8,128)S(1)} %stack.2), channel_id=1, replica_groups=mesh['depth'=32,'shot'=8] {'shot'}, dimensions={0} | all-to-all | bytes 1048576 | tf_op jit(solution)/shard_map/all_to_all | solution.py:145
  374.2 0.8 copy.52
  (71 shorter events, 2.8 us)
Async XLA Ops:
  7.2 236.6 %reduce-scatter.2.cloned.1.call-start = ((), (), s32[]{:S(2)}) async-start(), calls=%async_computation.2 | async-start | bytes 589824 | tf_op jit(solution)/shard_map/reduce_scatter | solution.py:98
  7.2 20.2 %copy-start.10 = (f32[1,16,64,128]{3,2,1,0:T(8,128)S(1)}, f32[1,16,64,128]{3,2,1,0:T(8,128)}, u32[]{:S(2)}) copy-start(f32[1,16,64,128]{3,2,1,0:T(8,128)} %param.19) | copy-start | bytes 1572868
  8.5 6.1 %copy-start.1 = (f32[1,16,64,128]{3,2,1,0:T(8,128)S(1)}, f32[1,16,64,128]{3,2,1,0:T(8,128)}, u32[]{:S(2)}) copy-start(f32[1,16,64,128]{3,2,1,0:T(8,128)} %param.18) | copy-start | bytes 1572868
  8.6 14.1 %copy-start.14 = (f32[1,4,256]{2,1,0:T(4,128)S(1)}, f32[1,4,256]{2,1,0:T(4,128)}, u32[]{:S(2)}) copy-start(f32[1,4,256]{2,1,0:T(4,128)} %param.24) | copy-start | bytes 12292
  8.6 14.1 %copy-start.15 = (s32[1,256]{1,0:T(1,128)S(1)}, s32[1,256]{1,0:T(1,128)}, u32[]{:S(2)}) copy-start(s32[1,256]{1,0:T(1,128)} %param.23) | copy-start | bytes 3076
  8.6 14.7 %copy-start.13 = (f32[1,4]{1,0:T(1,128)S(1)}, f32[1,4]{1,0:T(1,128)}, u32[]{:S(2)}) copy-start(f32[1,4]{1,0:T(1,128)} %param.22) | copy-start | bytes 52
  8.6 18.1 %copy-start.16 = (s32[3]{0:T(128)S(1)}, s32[3]{0:T(128)}, u32[]{:S(2)}) copy-start(s32[3]{0:T(128)} %constant.255.clone.1) | copy-start | bytes 40
  8.6 18.8 %copy-start.2 = (f32[1,16,64,128]{3,2,1,0:T(8,128)S(1)}, f32[1,16,64,128]{3,2,1,0:T(8,128)}, u32[]{:S(2)}) copy-start(f32[1,16,64,128]{3,2,1,0:T(8,128)} %param.20) | copy-start | bytes 1572868
  8.6 18.8 %collective-permute-start = (f32[4,64,128]{2,1,0:T(8,128)S(1)}, f32[4,64,128]{2,1,0:T(8,128)S(1)}, u32[]{:S(2)}, u32[]{:S(2)}) collective-permute-start(f32[4,64,128]{2,1,0:T(8,128)S(1)} %get-tuple-element.70), channel_id=1, source_target_pairs={{8,0},{16,8},{24,16},{32,24},{40,32},{48,40},{56,48},{64,56},{72,6... | collective-permute-start | bytes 393224 | tf_op jit(solution)/shard_map/ppermute | solution.py:21
  12.7 14.7 %collective-permute-start.1 = (f32[4,64,128]{2,1,0:T(8,128)S(1)}, f32[4,64,128]{2,1,0:T(8,128)S(1)}, u32[]{:S(2)}, u32[]{:S(2)}) collective-permute-start(f32[4,64,128]{2,1,0:T(8,128)S(1)} %get-tuple-element.71), channel_id=1, source_target_pairs={{0,8},{8,16},{16,24},{24,32},{32,40},{40,48},{48,56},{56,64},{64,7... | collective-permute-start | bytes 393224 | tf_op jit(solution)/shard_map/ppermute | solution.py:19
  14.7 38.7 %collective-permute-start.2 = (f32[4,64,128]{2,1,0:T(8,128)S(1)}, f32[4,64,128]{2,1,0:T(8,128)S(1)}, u32[]{:S(2)}, u32[]{:S(2)}) collective-permute-start(f32[4,64,128]{2,1,0:T(8,128)S(1)} %get-tuple-element.68), channel_id=1, source_target_pairs={{8,0},{16,8},{24,16},{32,24},{40,32},{48,40},{56,48},{64,56},{72,6... | collective-permute-start | bytes 393224 | tf_op jit(solution)/shard_map/ppermute | solution.py:21
  20.7 32.6 %collective-permute-start.3 = (f32[4,64,128]{2,1,0:T(8,128)S(1)}, f32[4,64,128]{2,1,0:T(8,128)S(1)}, u32[]{:S(2)}, u32[]{:S(2)}) collective-permute-start(f32[4,64,128]{2,1,0:T(8,128)S(1)} %get-tuple-element.69), channel_id=1, source_target_pairs={{0,8},{8,16},{16,24},{24,32},{32,40},{40,48},{48,56},{56,64},{64,7... | collective-permute-start | bytes 393224 | tf_op jit(solution)/shard_map/ppermute | solution.py:19
  29.4 24.0 %copy-start = (f32[16,64,128]{2,1,0:T(8,128)S(1)}, f32[16,64,128]{2,1,0:T(8,128)}, u32[]{:S(2)}) copy-start(f32[16,64,128]{2,1,0:T(8,128)} %param.16) | copy-start | bytes 1572868
  57.0 19.4 %copy-start.6 = (f32[16,64,128]{2,1,0:T(8,128)}, f32[16,64,128]{2,1,0:T(8,128)S(1)}, u32[]{:S(2)}) copy-start(f32[16,64,128]{2,1,0:T(8,128)S(1)} %get-tuple-element.61) | copy-start | bytes 1572868
  59.8 16.6 %collective-permute-start.10 = (f32[4,64,128]{2,1,0:T(8,128)S(1)}, f32[4,64,128]{2,1,0:T(8,128)S(1)}, u32[]{:S(2)}, u32[]{:S(2)}) collective-permute-start(f32[4,64,128]{2,1,0:T(8,128)S(1)} %get-tuple-element.59), channel_id=1, source_target_pairs={{8,0},{16,8},{24,16},{32,24},{40,32},{48,40},{56,48},{64,56},{72,6... | collective-permute-start | bytes 393224 | tf_op jit(solution)/shard_map/ppermute | solution.py:21
  65.9 10.6 %collective-permute-start.11 = (f32[4,64,128]{2,1,0:T(8,128)S(1)}, f32[4,64,128]{2,1,0:T(8,128)S(1)}, u32[]{:S(2)}, u32[]{:S(2)}) collective-permute-start(f32[4,64,128]{2,1,0:T(8,128)S(1)} %get-tuple-element.60), channel_id=1, source_target_pairs={{0,8},{8,16},{16,24},{24,32},{32,40},{40,48},{48,56},{56,64},{64,7... | collective-permute-start | bytes 393224 | tf_op jit(solution)/shard_map/ppermute | solution.py:19
  68.5 32.4 %collective-permute-start.4 = (f32[4,64,128]{2,1,0:T(8,128)}, f32[4,64,128]{2,1,0:T(8,128)S(1)}, u32[]{:S(2)}, u32[]{:S(2)}) collective-permute-start(f32[4,64,128]{2,1,0:T(8,128)} %get-tuple-element.66), channel_id=1, source_target_pairs={{8,0},{16,8},{24,16},{32,24},{40,32},{48,40},{56,48},{64,56},{72,6... | collective-permute-start | bytes 393224 | tf_op jit(solution)/shard_map/ppermute | solution.py:21
  74.5 26.3 %collective-permute-start.5 = (f32[4,64,128]{2,1,0:T(8,128)S(1)}, f32[4,64,128]{2,1,0:T(8,128)S(1)}, u32[]{:S(2)}, u32[]{:S(2)}) collective-permute-start(f32[4,64,128]{2,1,0:T(8,128)S(1)} %get-tuple-element.67), channel_id=1, source_target_pairs={{0,8},{8,16},{16,24},{24,32},{32,40},{40,48},{48,56},{56,64},{64,7... | collective-permute-start | bytes 393224 | tf_op jit(solution)/shard_map/ppermute | solution.py:19
  103.6 9.3 %copy-start.7 = (f32[16,64,128]{2,1,0:T(8,128)}, f32[16,64,128]{2,1,0:T(8,128)S(1)}, u32[]{:S(2)}) copy-start(f32[16,64,128]{2,1,0:T(8,128)S(1)} %get-tuple-element.58) | copy-start | bytes 1572868
  103.6 19.4 %collective-permute-start.12 = (f32[4,64,128]{2,1,0:T(8,128)S(1)}, f32[4,64,128]{2,1,0:T(8,128)S(1)}, u32[]{:S(2)}, u32[]{:S(2)}) collective-permute-start(f32[4,64,128]{2,1,0:T(8,128)S(1)} %get-tuple-element.56), channel_id=1, source_target_pairs={{8,0},{16,8},{24,16},{32,24},{40,32},{48,40},{56,48},{64,56},{72,6... | collective-permute-start | bytes 393224 | tf_op jit(solution)/shard_map/ppermute | solution.py:21
  109.7 13.3 %collective-permute-start.13 = (f32[4,64,128]{2,1,0:T(8,128)S(1)}, f32[4,64,128]{2,1,0:T(8,128)S(1)}, u32[]{:S(2)}, u32[]{:S(2)}) collective-permute-start(f32[4,64,128]{2,1,0:T(8,128)S(1)} %get-tuple-element.57), channel_id=1, source_target_pairs={{0,8},{8,16},{16,24},{24,32},{32,40},{40,48},{48,56},{56,64},{64,7... | collective-permute-start | bytes 393224 | tf_op jit(solution)/shard_map/ppermute | solution.py:19
  114.3 10.7 %copy-start.3 = (f32[16,64,128]{2,1,0:T(8,128)}, f32[16,64,128]{2,1,0:T(8,128)S(1)}, u32[]{:S(2)}) copy-start(f32[16,64,128]{2,1,0:T(8,128)S(1)} %scatter-add.45) | copy-start | bytes 1572868
  114.3 8.7 %copy-start.8 = (f32[16,64,128]{2,1,0:T(8,128)S(1)}, f32[16,64,128]{2,1,0:T(8,128)}, u32[]{:S(2)}) copy-start(f32[16,64,128]{2,1,0:T(8,128)} %copy-done.7) | copy-start | bytes 1572868
  115.0 25.2 %collective-permute-start.6 = (f32[4,64,128]{2,1,0:T(8,128)}, f32[4,64,128]{2,1,0:T(8,128)S(1)}, u32[]{:S(2)}, u32[]{:S(2)}) collective-permute-start(f32[4,64,128]{2,1,0:T(8,128)} %get-tuple-element.64), channel_id=1, source_target_pairs={{8,0},{16,8},{24,16},{32,24},{40,32},{48,40},{56,48},{64,56},{72,6... | collective-permute-start | bytes 393224 | tf_op jit(solution)/shard_map/ppermute | solution.py:21
  121.1 19.2 %collective-permute-start.7 = (f32[4,64,128]{2,1,0:T(8,128)}, f32[4,64,128]{2,1,0:T(8,128)}, u32[]{:S(2)}, u32[]{:S(2)}) collective-permute-start(f32[4,64,128]{2,1,0:T(8,128)} %get-tuple-element.65), channel_id=1, source_target_pairs={{0,8},{8,16},{16,24},{24,32},{32,40},{40,48},{48,56},{56,64},{64,7... | collective-permute-start | bytes 393224 | tf_op jit(solution)/shard_map/ppermute | solution.py:19
  150.8 9.5 %copy-start.4 = (f32[16,64,128]{2,1,0:T(8,128)}, f32[16,64,128]{2,1,0:T(8,128)S(1)}, u32[]{:S(2)}) copy-start(f32[16,64,128]{2,1,0:T(8,128)S(1)} %get-tuple-element.55) | copy-start | bytes 1572868
  150.9 19.6 %collective-permute-start.14 = (f32[4,64,128]{2,1,0:T(8,128)S(1)}, f32[4,64,128]{2,1,0:T(8,128)S(1)}, u32[]{:S(2)}, u32[]{:S(2)}) collective-permute-start(f32[4,64,128]{2,1,0:T(8,128)S(1)} %get-tuple-element.53), channel_id=1, source_target_pairs={{8,0},{16,8},{24,16},{32,24},{40,32},{48,40},{56,48},{64,56},{72,6... | collective-permute-start | bytes 393224 | tf_op jit(solution)/shard_map/ppermute | solution.py:21
  156.9 13.5 %collective-permute-start.15 = (f32[4,64,128]{2,1,0:T(8,128)S(1)}, f32[4,64,128]{2,1,0:T(8,128)}, u32[]{:S(2)}, u32[]{:S(2)}) collective-permute-start(f32[4,64,128]{2,1,0:T(8,128)S(1)} %get-tuple-element.54), channel_id=1, source_target_pairs={{0,8},{8,16},{16,24},{24,32},{32,40},{40,48},{48,56},{56,64},{64,7... | collective-permute-start | bytes 393224 | tf_op jit(solution)/shard_map/ppermute | solution.py:19
  161.7 8.7 %copy-start.5 = (f32[16,64,128]{2,1,0:T(8,128)S(1)}, f32[16,64,128]{2,1,0:T(8,128)}, u32[]{:S(2)}) copy-start(f32[16,64,128]{2,1,0:T(8,128)} %copy-done.4) | copy-start | bytes 1572868
  162.4 25.5 %collective-permute-start.8 = (f32[4,64,128]{2,1,0:T(8,128)}, f32[4,64,128]{2,1,0:T(8,128)S(1)}, u32[]{:S(2)}, u32[]{:S(2)}) collective-permute-start(f32[4,64,128]{2,1,0:T(8,128)} %get-tuple-element.62), channel_id=1, source_target_pairs={{8,0},{16,8},{24,16},{32,24},{40,32},{48,40},{56,48},{64,56},{72,6... | collective-permute-start | bytes 393224 | tf_op jit(solution)/shard_map/ppermute | solution.py:21
  168.5 19.4 %collective-permute-start.9 = (f32[4,64,128]{2,1,0:T(8,128)}, f32[4,64,128]{2,1,0:T(8,128)S(1)}, u32[]{:S(2)}, u32[]{:S(2)}) collective-permute-start(f32[4,64,128]{2,1,0:T(8,128)} %get-tuple-element.63), channel_id=1, source_target_pairs={{0,8},{8,16},{16,24},{24,32},{32,40},{40,48},{48,56},{56,64},{64,7... | collective-permute-start | bytes 393224 | tf_op jit(solution)/shard_map/ppermute | solution.py:19
  244.6 111.4 %copy-start.12 = (f32[16,8,128]{2,1,0:T(8,128)}, f32[16,8,128]{2,1,0:T(8,128)S(1)}, u32[]{:S(2)}) copy-start(f32[16,8,128]{2,1,0:T(8,128)S(1)} %broadcast_multiply_fusion) | copy-start | bytes 196612
  244.6 115.1 %copy-start.9 = (f32[2,5,16,8,128]{4,3,2,1,0:T(8,128)S(1)}, f32[2,5,16,8,128]{4,3,2,1,0:T(8,128)}, u32[]{:S(2)}) copy-start(f32[2,5,16,8,128]{4,3,2,1,0:T(8,128)} %param.25) | copy-start | bytes 1966084
  244.6 115.1 %copy-start.11 = (f32[16,8,128]{2,1,0:T(8,128)S(1)}, f32[16,8,128]{2,1,0:T(8,128)}, u32[]{:S(2)}) copy-start(f32[16,8,128]{2,1,0:T(8,128)} %reduce-scatter.2.cloned.1.call-done) | copy-start | bytes 196612
Sparse Core Ops, SparseCore 0:
  192.0 51.6 reduce-scatter.1
